TPU v7x, 32 devices: a whole 2x2x4 slice. The times are simulated.
32 devices in a mesh: dp: 8 (over y, x, core), expert: 4 (over z).
Axes of the slice: x: 2, y: 2, z: 4, core: 2. Of those that a mesh axis runs over, the one named last changes fastest.
Arguments:
- tokens: bfloat16 [4096, 1536], P(('dp', 'expert')), may hold values from -6 to 6
- segment_ids: int32 [32, 128], P(('dp', 'expert')), may hold values from 0 to 3, never falling along the last dimension, each value on 1 to 64 neighbouring positions
- routes: int32 [4096, 8], P(('dp', 'expert')), may hold values from 0 to 19, as said below
- cotangent: bfloat16 [4096, 1536], P(('dp', 'expert')), may hold values from -6 to 6
- query_weight: bfloat16 [1536, 1536], P('dp'), may hold values from -0.15625 to 0.15625
- key_weight: bfloat16 [1536, 512], P('dp'), may hold values from -0.15625 to 0.15625
- value_matrix: bfloat16 [1536, 512], P('dp'), may hold values from -0.15625 to 0.15625
- out_weight: bfloat16 [1536, 1536], P('dp'), may hold values from -1.25 to 1.25
- first_gain: bfloat16 [1536], P('dp'), may hold values from 0.5 to 1.5
- second_gain: bfloat16 [1536], P('dp'), may hold values from 0.5 to 1.5
- router_weight: bfloat16 [1536, 20], P('dp'), may hold values from -0.078125 to 0.078125
- gate_weight: bfloat16 [20, 1536, 512], P('expert'), may hold values from -0.15625 to 0.15625
- up_weight: bfloat16 [20, 1536, 512], P('expert'), may hold values from -0.15625 to 0.15625
- down_weight: bfloat16 [20, 512, 1536], P('expert'), may hold values from -0.5 to 0.5
Outputs:
- layer_out: bfloat16 [4096, 1536], P(('dp', 'expert'))
- input_grad: float32 [4096, 1536], P(('dp', 'expert'))
- query_grad: float32 [1536, 1536], P('dp')
- key_grad: float32 [1536, 512], P('dp')
- value_grad: float32 [1536, 512], P('dp')
- out_grad: float32 [1536, 1536], P('dp')
- first_grad: float32 [1536], P('dp')
- second_grad: float32 [1536], P('dp')
- router_grad: float32 [1536, 20], P('dp')
- gate_grad: float32 [20, 1536, 512], P('expert', 'dp')
- up_grad: float32 [20, 1536, 512], P('expert', 'dp')
- down_grad: float32 [20, 512, 1536], P('expert', 'dp')
Inputs may be any that keep to these rules, and one draw needn't show every extreme that they name: `segment_ids`: within each row the segment ids start at 0, never fall and take 4 values; a sequence has at most 64 tokens and some sequence has exactly that many. `routes`: each token names 8 different experts. Among the 128 tokens of one device no expert is named more than 96 times; in every such block between four and eight experts are named exactly 96 times.
All inputs are finite; a program needn't handle non-finite values.
Results may differ from a plain program's by a relative error of at most 0.012.
Values may be sent and summed in bfloat16 or wider, within the bound.
No kernel may reach another device: no remote copies, remote signals or barrier semaphores. Data moves between devices by JAX's collectives and lax.ppermute only.
A program may use at most 256 MiB of HBM per device.

v0:
```python
import jax
import jax.numpy as jnp
from jax import lax
from jax.sharding import PartitionSpec as P

HEAD_SIZE = 64
CAP = 96
EPSILON = 1e-06
ROTARY_BASE = 10000.0
SCORE_FACTOR = 0.015625
HIGHEST = lax.Precision.HIGHEST


def rope_tables(positions, width):
    half = width // 2
    freq = ROTARY_BASE ** (-jnp.arange(half, dtype=jnp.float32) * 2.0 / width)
    angle = positions.astype(jnp.float32)[:, None] * freq[None, :]
    return (jnp.cos(angle)[:, None, :], jnp.sin(angle)[:, None, :])


def rotate(field, cosine, sine):
    half = field.shape[-1] // 2
    first, second = (field[..., :half], field[..., half:])
    return jnp.concatenate(
        [first * cosine - second * sine, second * cosine + first * sine], axis=-1
    )


def rotate_back(grad, cosine, sine):
    half = grad.shape[-1] // 2
    first, second = (grad[..., :half], grad[..., half:])
    return jnp.concatenate(
        [first * cosine + second * sine, second * cosine - first * sine], axis=-1
    )


def positions_of(segments):
    count = segments.shape[0]
    earlier = jnp.sum((segments[None, :] < segments[:, None]).astype(jnp.int32), axis=1)
    return jnp.arange(count, dtype=jnp.int32) - earlier


def attention_mask(segments):
    count = segments.shape[0]
    index = jnp.arange(count, dtype=jnp.int32)
    return (segments[:, None] == segments[None, :]) & (index[None, :] <= index[:, None])


def rms_forward(field, gain):
    inverse = lax.rsqrt(jnp.mean(field * field, axis=-1, keepdims=True) + EPSILON)
    return (inverse, field * inverse * gain.astype(jnp.float32))


def rms_backward(field, inverse, gain, grad):
    scaled = grad * gain.astype(jnp.float32)
    inner = jnp.mean(scaled * field, axis=-1, keepdims=True)
    return (inverse * scaled - field * inverse**3 * inner, jnp.sum(grad * field * inverse, axis=0))


def score_block(query_rows, key_rows, mask):
    score_matrix = (
        jnp.einsum("qean,wen->eaqw", query_rows, key_rows, preferred_element_type=jnp.float32)
        * SCORE_FACTOR
    )
    return jnp.where(mask[None, None], score_matrix, -1e30)


def expert_front(arrived, gate_weight, up_weight):
    gate_pre = jnp.einsum("erd,edh->erh", arrived, gate_weight, preferred_element_type=jnp.float32)
    up_pre = jnp.einsum("erd,edh->erh", arrived, up_weight, preferred_element_type=jnp.float32)
    hidden = (jax.nn.silu(gate_pre) * up_pre).astype(jnp.bfloat16)
    return (gate_pre, up_pre, hidden)


def local(
    tokens,
    segment_ids,
    routes,
    cotangent,
    query_weight,
    key_weight,
    value_matrix,
    out_weight,
    first_gain,
    second_gain,
    router_weight,
    gate_weight,
    up_weight,
    down_weight,
):
    gathered = (
        lax.all_gather(query_weight, "dp", axis=0, tiled=True),
        lax.all_gather(key_weight, "dp", axis=0, tiled=True),
        lax.all_gather(value_matrix, "dp", axis=0, tiled=True),
        lax.all_gather(out_weight, "dp", axis=0, tiled=True),
        lax.all_gather(first_gain, "dp", axis=0, tiled=True),
        lax.all_gather(second_gain, "dp", axis=0, tiled=True),
        lax.all_gather(router_weight, "dp", axis=0, tiled=True),
    )
    query_full, key_full, value_full, out_full, gain_one, gain_two, router_full = gathered
    token_rows, width = tokens.shape
    query_head_rows = query_full.shape[1] // HEAD_SIZE
    key_heads = key_full.shape[1] // HEAD_SIZE
    head_group = query_head_rows // key_heads
    experts = router_full.shape[1]
    choices_per = routes.shape[1]
    segments = segment_ids[0]
    mask = attention_mask(segments)
    cosine, sine = rope_tables(positions_of(segments), HEAD_SIZE)
    inputs = tokens.astype(jnp.float32)
    first_inverse, normed1 = rms_forward(inputs, gain_one)
    normed1 = normed1.astype(jnp.bfloat16)
    query_rows = rotate(
        jnp.dot(normed1, query_full, preferred_element_type=jnp.float32).reshape(
            token_rows, query_head_rows, HEAD_SIZE
        ),
        cosine,
        sine,
    )
    query_rows = query_rows.astype(jnp.bfloat16).reshape(
        token_rows, key_heads, head_group, HEAD_SIZE
    )
    key_rows = rotate(
        jnp.dot(normed1, key_full, preferred_element_type=jnp.float32).reshape(
            token_rows, key_heads, HEAD_SIZE
        ),
        cosine,
        sine,
    ).astype(jnp.bfloat16)
    value_rows = (
        jnp.dot(normed1, value_full, preferred_element_type=jnp.float32)
        .astype(jnp.bfloat16)
        .reshape(token_rows, key_heads, HEAD_SIZE)
    )
    score_matrix = score_block(query_rows, key_rows, mask)
    peak = jnp.max(score_matrix, axis=-1, keepdims=True)
    logsum = peak + jnp.log(jnp.sum(jnp.exp(score_matrix - peak), axis=-1, keepdims=True))
    probabilities = jnp.exp(score_matrix - logsum).astype(jnp.bfloat16)
    mixed_values = jnp.einsum(
        "wmik,kwy->iwmy", probabilities, value_rows, preferred_element_type=jnp.float32
    )
    mixed_values = mixed_values.astype(jnp.bfloat16).reshape(
        token_rows, query_head_rows * HEAD_SIZE
    )
    resid = inputs + jnp.dot(mixed_values, out_full, preferred_element_type=jnp.float32)
    second_inverse, normed2 = rms_forward(resid, gain_two)
    normed2 = normed2.astype(jnp.bfloat16)
    logits = jnp.dot(normed2, router_full, preferred_element_type=jnp.float32)
    choose = (routes[:, :, None] == jnp.arange(experts, dtype=jnp.int32)[None, None, :]).astype(
        jnp.float32
    )
    chosen = jnp.sum(choose * logits[:, None, :], axis=-1)
    top = jnp.max(chosen, axis=-1, keepdims=True)
    raised = jnp.exp(chosen - top)
    gates = raised / jnp.sum(raised, axis=-1, keepdims=True)
    flat = routes.reshape(-1)
    hits = (flat[:, None] == jnp.arange(experts, dtype=jnp.int32)[None, :]).astype(jnp.int32)
    slots = jnp.sum((jnp.cumsum(hits, axis=0) - hits) * hits, axis=1)
    empty = jnp.zeros((experts, CAP, width), jnp.bfloat16)
    outgoing = empty.at[flat, slots].set(jnp.repeat(normed2, choices_per, axis=0))
    arrived = lax.all_to_all(outgoing, "expert", split_axis=0, concat_axis=1, tiled=True)
    gate_pre, up_pre, hidden = expert_front(arrived, gate_weight, up_weight)
    produced = jnp.einsum(
        "erh,ehd->erd", hidden, down_weight, preferred_element_type=jnp.float32
    ).astype(jnp.bfloat16)
    returned = lax.all_to_all(produced, "expert", split_axis=1, concat_axis=0, tiled=True)
    picked = returned[flat, slots].reshape(token_rows, choices_per, width)
    combined = jnp.einsum("tk,tkd->td", gates, picked.astype(jnp.float32), precision=HIGHEST)
    layer_out = (resid + combined).astype(jnp.bfloat16)
    grad_out = cotangent.astype(jnp.float32)
    gate_back = jnp.einsum("td,tkd->tk", cotangent, picked, preferred_element_type=jnp.float32)
    chosen_back = gates * (gate_back - jnp.sum(gates * gate_back, axis=-1, keepdims=True))
    logit_back = jnp.sum(choose * chosen_back[:, :, None], axis=1)
    router_part = jnp.dot(normed2.astype(jnp.float32).T, logit_back, precision=HIGHEST)
    normed2_back = jnp.dot(logit_back, router_full.astype(jnp.float32).T, precision=HIGHEST)
    row_grads = (
        (gates[:, :, None] * grad_out[:, None, :])
        .astype(jnp.bfloat16)
        .reshape(token_rows * choices_per, width)
    )
    leaving = empty.at[flat, slots].set(row_grads)
    incoming = lax.all_to_all(leaving, "expert", split_axis=0, concat_axis=1, tiled=True)
    landed, gate_again, up_again, hidden_again = (arrived, gate_pre, up_pre, hidden)
    hidden_back = jnp.einsum(
        "erd,ehd->erh", incoming, down_weight, preferred_element_type=jnp.float32
    )
    sigma = jax.nn.sigmoid(gate_again)
    gate_rows = (hidden_back * up_again * sigma * (1.0 + gate_again * (1.0 - sigma))).astype(
        jnp.bfloat16
    )
    up_rows = (hidden_back * gate_again * sigma).astype(jnp.bfloat16)
    down_part = jnp.einsum(
        "erh,erd->ehd", hidden_again, incoming, preferred_element_type=jnp.float32
    )
    gate_part = jnp.einsum("erd,erh->edh", landed, gate_rows, preferred_element_type=jnp.float32)
    up_part = jnp.einsum("erd,erh->edh", landed, up_rows, preferred_element_type=jnp.float32)
    rows_back = jnp.einsum(
        "erh,edh->erd", gate_rows, gate_weight, preferred_element_type=jnp.float32
    )
    rows_back = (
        rows_back
        + jnp.einsum("erh,edh->erd", up_rows, up_weight, preferred_element_type=jnp.float32)
    ).astype(jnp.bfloat16)
    expert_sums = (gate_part, up_part, down_part)
    coming_back = lax.all_to_all(rows_back, "expert", split_axis=1, concat_axis=0, tiled=True)
    normed2_back = normed2_back + jnp.sum(
        coming_back[flat, slots].reshape(token_rows, choices_per, width).astype(jnp.float32), axis=1
    )
    resid_part, second_part = rms_backward(resid, second_inverse, gain_two, normed2_back)
    resid_back = grad_out + resid_part
    attended_back = resid_back.astype(jnp.bfloat16)
    out_part = jnp.dot(mixed_values.T, attended_back, preferred_element_type=jnp.float32)
    mixed_values_gradient = jnp.dot(
        attended_back, out_full.T, preferred_element_type=jnp.float32
    ).astype(jnp.bfloat16)
    mixed_values_gradient = mixed_values_gradient.reshape(
        token_rows, key_heads, head_group, HEAD_SIZE
    )
    second_pass = jnp.exp(score_block(query_rows, key_rows, mask) - logsum)
    value_rows_gradient = jnp.einsum(
        "kjal,akjx->lkx",
        second_pass.astype(jnp.bfloat16),
        mixed_values_gradient,
        preferred_element_type=jnp.float32,
    )
    probability_gradient = jnp.einsum(
        "qean,wen->eaqw", mixed_values_gradient, value_rows, preferred_element_type=jnp.float32
    )
    delta = jnp.sum(second_pass * probability_gradient, axis=-1, keepdims=True)
    score_gradient = (second_pass * (probability_gradient - delta) * SCORE_FACTOR).astype(
        jnp.bfloat16
    )
    query_rows_gradient = jnp.einsum(
        "wmik,kwy->iwmy", score_gradient, key_rows, preferred_element_type=jnp.float32
    ).reshape(token_rows, query_head_rows, HEAD_SIZE)
    key_rows_gradient = jnp.einsum(
        "kjal,akjx->lkx", score_gradient, query_rows, preferred_element_type=jnp.float32
    )
    query_rows_gradient = (
        rotate_back(query_rows_gradient, cosine, sine)
        .astype(jnp.bfloat16)
        .reshape(token_rows, query_head_rows * HEAD_SIZE)
    )
    key_rows_gradient = (
        rotate_back(key_rows_gradient, cosine, sine)
        .astype(jnp.bfloat16)
        .reshape(token_rows, key_heads * HEAD_SIZE)
    )
    value_rows_gradient = value_rows_gradient.astype(jnp.bfloat16).reshape(
        token_rows, key_heads * HEAD_SIZE
    )
    query_part = jnp.dot(normed1.T, query_rows_gradient, preferred_element_type=jnp.float32)
    key_part = jnp.dot(normed1.T, key_rows_gradient, preferred_element_type=jnp.float32)
    value_part = jnp.dot(normed1.T, value_rows_gradient, preferred_element_type=jnp.float32)
    normed1_back = jnp.dot(query_rows_gradient, query_full.T, preferred_element_type=jnp.float32)
    normed1_back = normed1_back + jnp.dot(
        key_rows_gradient, key_full.T, preferred_element_type=jnp.float32
    )
    normed1_back = normed1_back + jnp.dot(
        value_rows_gradient, value_full.T, preferred_element_type=jnp.float32
    )
    input_part, first_part = rms_backward(inputs, first_inverse, gain_one, normed1_back)
    input_grad = resid_back + input_part
    partial_sums = (
        lax.psum_scatter(query_part, "dp", scatter_dimension=0, tiled=True),
        lax.psum_scatter(key_part, "dp", scatter_dimension=0, tiled=True),
        lax.psum_scatter(value_part, "dp", scatter_dimension=0, tiled=True),
        lax.psum_scatter(out_part, "dp", scatter_dimension=0, tiled=True),
        lax.psum_scatter(first_part, "dp", scatter_dimension=0, tiled=True),
        lax.psum_scatter(second_part, "dp", scatter_dimension=0, tiled=True),
        lax.psum_scatter(router_part, "dp", scatter_dimension=0, tiled=True),
    )
    totals = lax.psum(
        (
            partial_sums[0],
            partial_sums[1],
            partial_sums[2],
            partial_sums[3],
            partial_sums[4],
            partial_sums[5],
            partial_sums[6],
        ),
        "expert",
    )
    expert_sums = (
        lax.psum_scatter(gate_part, "dp", scatter_dimension=1, tiled=True),
        lax.psum_scatter(up_part, "dp", scatter_dimension=1, tiled=True),
        lax.psum_scatter(down_part, "dp", scatter_dimension=1, tiled=True),
    )
    return (
        layer_out,
        input_grad,
        totals[0],
        totals[1],
        totals[2],
        totals[3],
        totals[4],
        totals[5],
        totals[6],
        expert_sums[0],
        expert_sums[1],
        expert_sums[2],
    )


def solution(mesh):
    return jax.shard_map(
        local,
        mesh=mesh,
        in_specs=(
            P(("dp", "expert"), None),
            P(("dp", "expert"), None),
            P(("dp", "expert"), None),
            P(("dp", "expert"), None),
            P("dp", None),
            P("dp", None),
            P("dp", None),
            P("dp", None),
            P("dp"),
            P("dp"),
            P("dp", None),
            P("expert", None, None),
            P("expert", None, None),
            P("expert", None, None),
        ),
        out_specs=(
            P(("dp", "expert"), None),
            P(("dp", "expert"), None),
            P("dp", None),
            P("dp", None),
            P("dp", None),
            P("dp", None),
            P("dp"),
            P("dp"),
            P("dp", None),
            P("expert", "dp", None),
            P("expert", "dp", None),
            P("expert", "dp", None),
        ),
        check_vma=False,
    )
```

profile of v0, /device:TPU:0, one launch (start us, length us, event | category | flops | bytes accessed | tf_op | source)
XLA Modules:
  0.0 1799.5 jit_solution(2375361750178085493)
XLA Ops:
  14.8 15.5 all-reduce.7
  40.5 25.7 %all-gather.8.cloned.1.call-done = bf16[1536,512]{1,0:T(8,128)(2,1)} async-done(((bf16[192,512]{1,0:T(8,128)(2,1)}), bf16[1536,512]{1,0:T(8,128)(2,1)}) %all-gather.8.cloned.1.call-update) | async-done | bytes 1572880 | tf_op jit(solution)/shard_map/all_gather | solution.py:93
  68.4 38.6 %all-gather.10.cloned.1.call-done = bf16[1536,1536]{1,0:T(8,128)(2,1)} async-done(((bf16[192,1536]{1,0:T(8,128)(2,1)}), bf16[1536,1536]{1,0:T(8,128)(2,1)}) %all-gather.10.cloned.1.call-update) | async-done | bytes 4718608 | tf_op jit(solution)/shard_map/all_gather | solution.py:92
  114.2 33.5 %all-gather.12.cloned.1.call-done = bf16[1536,1536]{1,0:T(8,128)(2,1)} async-done(((bf16[192,1536]{1,0:T(8,128)(2,1)}), bf16[1536,1536]{1,0:T(8,128)(2,1)}) %all-gather.12.cloned.1.call-update) | async-done | bytes 4718608 | tf_op jit(solution)/shard_map/all_gather | solution.py:95
  152.0 9.5 scatter_custom_fusion
  161.5 134.7 %all_to_all.72 = bf16[20,96,1536]{2,1,0:T(8,128)(2,1)S(1)} all-to-all(bf16[20,96,1536]{2,1,0:T(8,128)(2,1)} %bitcast.191), channel_id=1, replica_groups=mesh['dp'=8,'expert'=4] {'expert'}, dimensions={0} | all-to-all | bytes 11796480 | tf_op jit(solution)/shard_map/all_to_all | solution.py:161
  296.7 10.8 fusion.76
  323.1 10.0 copy.108
  339.1 9.3 all-gather
  350.4 193.8 %all-to-all-done.1 = bf16[5,384,1536]{2,0,1:T(8,128)(2,1)} async-done(((bf16[5,384,1536]{2,0,1:T(8,128)(2,1)}), bf16[5,384,1536]{2,0,1:T(8,128)(2,1)}, u32[]{:S(2)}, u32[]{:S(2)}) %all-to-all-start.1) | async-done | bytes 5898272 | tf_op jit(solution)/shard_map/all_to_all | solution.py:166
  552.7 17.8 gather_fusion
  576.6 9.6 scatter_custom_fusion.1
  586.2 133.4 %all_to_all.73 = bf16[20,96,1536]{2,1,0:T(8,128)(2,1)S(1)} all-to-all(bf16[20,96,1536]{2,1,0:T(8,128)(2,1)} %bitcast.188), channel_id=1, replica_groups=mesh['dp'=8,'expert'=4] {'expert'}, dimensions={0} | all-to-all | bytes 11796480 | tf_op jit(solution)/shard_map/all_to_all | solution.py:182
  722.7 12.6 multiply_convert_fusion
  735.3 11.2 fusion.77
  746.5 13.0 add_convert_fusion
  759.5 10.0 copy.112
  781.5 198.6 %all-to-all-done.3 = bf16[5,384,1536]{2,0,1:T(8,128)(2,1)} async-done(((bf16[5,384,1536]{2,0,1:T(8,128)(2,1)}), bf16[5,384,1536]{2,0,1:T(8,128)(2,1)}, u32[]{:S(2)}, u32[]{:S(2)}) %all-to-all-start.3) | async-done | bytes 5898272 | tf_op jit(solution)/shard_map/all_to_all | solution.py:205
  988.5 23.3 %gather_fusion.1 = bf16[1024,1536]{1,0:T(8,128)(2,1)} fusion(bf16[20,96,1536]{2,1,0:T(8,128)(2,1)} %bitcast.181, s32[1024]{0:T(1024)S(1)} %bitcast.179), kind=kCustom, calls=%fused_computation.1 | custom fusion | bytes 6299648 | tf_op jit(solution)/shard_map/gather | solution.py:207
  1060.3 13.1 fusion.83
  1073.6 13.9 fusion.82
  1087.5 11.3 fusion.81
  1099.0 24.6 %reduce-scatter.13.cloned.1.call-done = f32[192,512]{1,0:T(8,128)} async-done(((f32[1536,512]{1,0:T(8,128)}), f32[192,512]{1,0:T(8,128)}) %reduce-scatter.13.cloned.1.call-update) | async-done | bytes 393232 | tf_op jit(solution)/shard_map/reduce_scatter | solution.py:266
  1123.6 80.0 %reduce-scatter.17.cloned.1.call-done = f32[192,1536]{1,0:T(8,128)} async-done(((f32[1536,1536]{1,0:T(8,128)}), f32[192,1536]{1,0:T(8,128)}) %reduce-scatter.17.cloned.1.call-update) | async-done | bytes 1179664 | tf_op jit(solution)/shard_map/reduce_scatter | solution.py:268
  1203.6 80.0 %reduce-scatter.11.cloned.1.call-done = f32[192,1536]{1,0:T(8,128)} async-done(((f32[1536,1536]{1,0:T(8,128)}), f32[192,1536]{1,0:T(8,128)}) %reduce-scatter.11.cloned.1.call-update) | async-done | bytes 1179664 | tf_op jit(solution)/shard_map/reduce_scatter | solution.py:265
  1284.5 37.9 %reduce-scatter.25.cloned.1.call-done = f32[192,20]{1,0:T(8,128)} async-done(((f32[1536,20]{1,0:T(8,128)}), f32[192,20]{1,0:T(8,128)}) %reduce-scatter.25.cloned.1.call-update) | async-done | bytes 15376
  1329.1 22.8 %all-reduce.4 = (f32[1536]{0:T(1024)S(1)}, f32[1536]{0:T(1024)S(1)}) all-reduce(f32[1536]{0:T(1024)S(1)} %get-tuple-element.14, f32[1536]{0:T(1024)S(1)} %copy-done.47), channel_id=6, replica_groups=mesh['dp'=8,'expert'=4] {'dp'}, use_global_device_ids=true, to_apply=%region_28.29.clone | all-reduce | flops 3072 | bytes 24576
  1352.0 19.6 %all-reduce.5 = (f32[192]{0:T(256)}, f32[192]{0:T(256)}, f32[192,20]{0,1:T(8,128)}) all-reduce(f32[192]{0:T(256)S(1)} %dynamic-slice.3, f32[192]{0:T(256)S(1)} %dynamic-slice.5, f32[192,20]{0,1:T(8,128)S(1)} %copy.139), channel_id=1, replica_groups=mesh['dp'=8,'expert'=4] {'expert'}, use_global_device_ids=true, to_apply=%region_29.30 | all-reduce | flops 4224 | bytes 33792 | tf_op jit(solution)/shard_map/psum | solution.py:273
  1372.8 62.7 %reduce-scatter.23.cloned.1.call-done = f32[5,64,1536]{2,1,0:T(8,128)} async-done(((f32[5,512,1536]{2,1,0:T(8,128)}), f32[5,64,1536]{2,1,0:T(8,128)}) %reduce-scatter.23.cloned.1.call-update) | async-done | bytes 1966096 | tf_op jit(solution)/shard_map/reduce_scatter | solution.py:288
  1435.5 113.3 %reduce-scatter.21.cloned.1.call-done = f32[5,192,512]{2,1,0:T(8,128)} async-done(((f32[5,1536,512]{2,1,0:T(8,128)}), f32[5,192,512]{2,1,0:T(8,128)}) %reduce-scatter.21.cloned.1.call-update) | async-done | bytes 1966096 | tf_op jit(solution)/shard_map/reduce_scatter | solution.py:287
  1548.8 113.1 %reduce-scatter.19.cloned.1.call-done = f32[5,192,512]{2,1,0:T(8,128)} async-done(((f32[5,1536,512]{2,1,0:T(8,128)}), f32[5,192,512]{2,1,0:T(8,128)}) %reduce-scatter.19.cloned.1.call-update) | async-done | bytes 1966096 | tf_op jit(solution)/shard_map/reduce_scatter | solution.py:286
  1661.9 124.8 %all-reduce.10.cloned.1.call-done = (f32[192,1536]{1,0:T(8,128)}, f32[192,512]{1,0:T(8,128)}, f32[192,512]{1,0:T(8,128)}, f32[192,1536]{1,0:T(8,128)}) async-done(((f32[192,1536]{1,0:T(8,128)}, f32[192,512]{1,0:T(8,128)}, f32[192,512]{1,0:T(8,128)}, f32[192,1536]{1,0:T(8,128)}), (f32[192,1536]{1,0:T(8,128)}, f32[192,512]{1,0:T(8,128)}, f32[192,512]{1,0:T(8,128)}, ...) | async-done | bytes 3145744 | tf_op jit(solution)/shard_map/psum | solution.py:273
  (254 shorter events, 155.1 us)
Async XLA Ops:
  7.2 31.3 %all-gather.6.cloned.1.call-start = ((), (), s32[]{:S(2)}) async-start(), calls=%async_computation.12 | async-start | bytes 1769472 | tf_op jit(solution)/shard_map/all_gather | solution.py:94
  8.0 58.2 %all-gather.8.cloned.1.call-start = ((), (), s32[]{:S(2)}) async-start(), calls=%async_computation.13 | async-start | bytes 1769472 | tf_op jit(solution)/shard_map/all_gather | solution.py:93
  8.7 98.3 %all-gather.10.cloned.1.call-start = ((), (), s32[]{:S(2)}) async-start(), calls=%async_computation.14 | async-start | bytes 5308416 | tf_op jit(solution)/shard_map/all_gather | solution.py:92
  9.4 138.2 %all-gather.12.cloned.1.call-start = ((), (), s32[]{:S(2)}) async-start(), calls=%async_computation.15 | async-start | bytes 5308416 | tf_op jit(solution)/shard_map/all_gather | solution.py:95
  30.4 121.2 %copy-start.37 = (f32[1536]{0:T(1024)}, f32[1536]{0:T(1024)S(1)}, u32[]{:S(2)}) copy-start(f32[1536]{0:T(1024)S(1)} %convert_element_type.119) | copy-start | bytes 18436
  37.7 73.7 %copy-start.48 = (f32[128]{0:T(128)}, f32[128]{0:T(128)S(1)}, u32[]{:S(2)}) copy-start(f32[128]{0:T(128)S(1)} %get-tuple-element.49) | copy-start | bytes 1540
  37.7 114.3 %copy-start.54 = (s32[1024]{0:T(1024)}, s32[1024]{0:T(1024)S(1)}, u32[]{:S(2)}) copy-start(s32[1024]{0:T(1024)S(1)} %broadcast_select_fusion) | copy-start | bytes 12292
  37.9 73.5 %copy-start.26 = (f32[128,32]{0,1:T(8,128)}, f32[128,32]{0,1:T(8,128)S(1)}, u32[]{:S(2)}) copy-start(f32[128,32]{0,1:T(8,128)S(1)} %get-tuple-element.44) | copy-start | bytes 49156
  37.9 73.5 %copy-start.29 = (f32[128,32]{0,1:T(8,128)}, f32[128,32]{0,1:T(8,128)S(1)}, u32[]{:S(2)}) copy-start(f32[128,32]{0,1:T(8,128)S(1)} %get-tuple-element.45) | copy-start | bytes 49156
  40.5 72.5 %copy-start.20 = (bf16[128,512]{0,1:T(8,128)(2,1)}, bf16[128,512]{0,1:T(8,128)(2,1)S(1)}, u32[]{:S(2)}) copy-start(bf16[128,512]{0,1:T(8,128)(2,1)S(1)} %copy.97) | copy-start | bytes 393220
  68.4 43.1 %copy-start.40 = (bf16[128,8,32]{0,2,1:T(8,128)(2,1)}, bf16[128,8,32]{0,2,1:T(8,128)(2,1)S(1)}, u32[]{:S(2)}) copy-start(bf16[128,8,32]{0,2,1:T(8,128)(2,1)S(1)} %get-tuple-element.39) | copy-start | bytes 196612
  68.4 43.1 %copy-start.42 = (bf16[128,8,32]{0,2,1:T(8,128)(2,1)}, bf16[128,8,32]{0,2,1:T(8,128)(2,1)S(1)}, u32[]{:S(2)}) copy-start(bf16[128,8,32]{0,2,1:T(8,128)(2,1)S(1)} %get-tuple-element.40) | copy-start | bytes 196612
  114.2 36.7 %copy-start.9 = (bf16[8,64,3,128]{3,1,2,0:T(8,128)(2,1)}, bf16[8,64,3,128]{3,1,2,0:T(8,128)(2,1)S(1)}, u32[]{:S(2)}) copy-start(bf16[8,64,3,128]{3,1,2,0:T(8,128)(2,1)S(1)} %convolution_convert_fusion.2) | copy-start | bytes 1179652
  152.0 197.6 %copy-start.7 = (bf16[128,1536]{1,0:T(8,128)(2,1)}, bf16[128,1536]{1,0:T(8,128)(2,1)S(1)}, u32[]{:S(2)}) copy-start(bf16[128,1536]{1,0:T(8,128)(2,1)S(1)} %multiply_convert_fusion.3) | copy-start | bytes 1179652
  333.1 211.1 %all-to-all-start.1 = ((bf16[5,384,1536]{2,0,1:T(8,128)(2,1)}), bf16[5,384,1536]{2,0,1:T(8,128)(2,1)}, u32[]{:S(2)}, u32[]{:S(2)}) async-start(bf16[5,384,1536]{2,0,1:T(8,128)(2,1)} %copy.108), calls=%async_computation.1 | async-start | bytes 18874368 | tf_op jit(solution)/shard_map/all_to_all | solution.py:166
  348.6 204.1 %copy-start.24 = (bf16[1536,20]{0,1:T(8,128)(2,1)}, bf16[1536,20]{0,1:T(8,128)(2,1)S(1)}, u32[]{:S(2)}) copy-start(bf16[1536,20]{0,1:T(8,128)(2,1)S(1)} %reshape.368) | copy-start | bytes 184324
  349.8 202.9 %copy-start.53 = (f32[128]{0:T(128)}, f32[128]{0:T(128)S(1)}, u32[]{:S(2)}) copy-start(f32[128]{0:T(128)S(1)} %reduce_max.19) | copy-start | bytes 1540
  769.4 210.6 %all-to-all-start.3 = ((bf16[5,384,1536]{2,0,1:T(8,128)(2,1)}), bf16[5,384,1536]{2,0,1:T(8,128)(2,1)}, u32[]{:S(2)}, u32[]{:S(2)}) async-start(bf16[5,384,1536]{2,0,1:T(8,128)(2,1)} %copy.112), calls=%async_computation.3 | async-start | bytes 18874368 | tf_op jit(solution)/shard_map/all_to_all | solution.py:205
  775.4 323.6 %reduce-scatter.15.cloned.1.call-start = ((), (), s32[]{:S(2)}) async-start(), calls=%async_computation.18 | async-start | bytes 3538944 | tf_op jit(solution)/shard_map/reduce_scatter | solution.py:267
  776.0 239.9 %copy-start.39 = (f32[128,20]{0,1:T(8,128)}, f32[128,20]{0,1:T(8,128)S(1)}, u32[]{:S(2)}) copy-start(f32[128,20]{0,1:T(8,128)S(1)} %select_reduce_fusion) | copy-start | bytes 30724
  1029.3 94.4 %reduce-scatter.13.cloned.1.call-start = ((), (), s32[]{:S(2)}) async-start(), calls=%async_computation.17 | async-start | bytes 3538944 | tf_op jit(solution)/shard_map/reduce_scatter | solution.py:266
  1039.4 164.2 %reduce-scatter.17.cloned.1.call-start = ((), (), s32[]{:S(2)}) async-start(), calls=%async_computation.19 | async-start | bytes 10616832 | tf_op jit(solution)/shard_map/reduce_scatter | solution.py:268
  1044.5 239.2 %reduce-scatter.11.cloned.1.call-start = ((), (), s32[]{:S(2)}) async-start(), calls=%async_computation.16 | async-start | bytes 10616832 | tf_op jit(solution)/shard_map/reduce_scatter | solution.py:265
  1057.1 265.3 %reduce-scatter.25.cloned.1.call-start = ((), (), s32[]{:S(2)}) async-start(), calls=%async_computation.23 | async-start | bytes 884736
  1060.2 375.3 %reduce-scatter.23.cloned.1.call-start = ((), (), s32[]{:S(2)}) async-start(), calls=%async_computation.22 | async-start | bytes 17694720 | tf_op jit(solution)/shard_map/reduce_scatter | solution.py:288
  1073.3 475.4 %reduce-scatter.21.cloned.1.call-start = ((), (), s32[]{:S(2)}) async-start(), calls=%async_computation.21 | async-start | bytes 17694720 | tf_op jit(solution)/shard_map/reduce_scatter | solution.py:287
  1087.5 574.4 %reduce-scatter.19.cloned.1.call-start = ((), (), s32[]{:S(2)}) async-start(), calls=%async_computation.20 | async-start | bytes 17694720 | tf_op jit(solution)/shard_map/reduce_scatter | solution.py:286
  1098.9 224.5 %copy-start.12 = (bf16[128,24,64]{0,2,1:T(8,128)(2,1)S(1)}, bf16[128,24,64]{0,2,1:T(8,128)(2,1)}, u32[]{:S(2)}) copy-start(bf16[128,24,64]{0,2,1:T(8,128)(2,1)} %copy-done.11) | copy-start | bytes 1179652
  1098.9 687.8 %all-reduce.10.cloned.1.call-start = ((), (), s32[]{:S(2)}) async-start(), calls=%async_computation.24 | async-start | bytes 6291456 | tf_op jit(solution)/shard_map/psum | solution.py:273
  1283.7 43.9 %copy-start.6 = (bf16[1536,512]{1,0:T(8,128)(2,1)S(1)}, bf16[1536,512]{1,0:T(8,128)(2,1)}, u32[]{:S(2)}) copy-start(bf16[1536,512]{1,0:T(8,128)(2,1)} %all-gather.8.cloned.1.call-done) | copy-start | bytes 4718596
  1283.7 43.9 %copy-start.22 = (bf16[128,8,64]{0,2,1:T(8,128)(2,1)S(1)}, bf16[128,8,64]{0,2,1:T(8,128)(2,1)}, u32[]{:S(2)}) copy-start(bf16[128,8,64]{0,2,1:T(8,128)(2,1)} %copy-done.21) | copy-start | bytes 393220
  1327.6 44.0 %copy-start.59 = (f32[128]{0:T(128)S(1)}, f32[128]{0:T(128)}, u32[]{:S(2)}) copy-start(f32[128]{0:T(128)} %get-tuple-element.48) | copy-start | bytes 1540
  (45 other events, 319.8 us)
Sparse Core Ops, SparseCore 0:
  9.9 28.5 all-gather.5
  40.4 25.7 all-gather.7
  68.0 38.9 all-gather.9
  108.7 38.9 all-gather.11
  1029.4 44.3 reduce-scatter.14
  1077.4 46.2 reduce-scatter.12
  1127.1 76.4 reduce-scatter.16
  1207.1 76.4 reduce-scatter.10
  1287.4 34.9 reduce-scatter.24
  1326.3 109.1 reduce-scatter.22
  1439.6 109.1 reduce-scatter.20
  1552.7 109.1 reduce-scatter.18
  1664.5 122.1 all-reduce.9
where the time goes:
time: 1810 us; the launch traced here: 1800 us
  waiting for transfers between devices  1130 us (62%)
  blocking collectives  335 us (19%)
  matrix products  165 us (9%)
  local copies, waits for them, and re-layouts  112 us (6%)
  other arithmetic  27.9 us (2%)
    all_to_all x1, waiting for transfers between devices, local(): lax.all_to_all(rows_back, 'expert', split_axis=1, concat_axis=0, tiled=True)  199 us
    all_to_all x1, waiting for transfers between devices, local(): lax.all_to_all(produced, 'expert', split_axis=1, concat_axis=0, tiled=True)  194 us
    all_to_all x1, blocking collectives, local(): lax.all_to_all(outgoing, 'expert', split_axis=0, concat_axis=1, tiled=True)  135 us
    all_to_all x1, blocking collectives, local(): lax.all_to_all(leaving, 'expert', split_axis=0, concat_axis=1, tiled=True)  133 us
    psum x1, waiting for transfers between devices, local(): lax.psum((partial_sums[0], partial_sums[1], partial_sums[2], partial_sums...  125 us
    reduce_scatter x1, waiting for transfers between devices, local(): lax.psum_scatter(up_part, 'dp', scatter_dimension=1, tiled=True)  113 us
    reduce_scatter x1, waiting for transfers between devices, local(): lax.psum_scatter(gate_part, 'dp', scatter_dimension=1, tiled=True)  113 us
    reduce_scatter x1, waiting for transfers between devices, local(): lax.psum_scatter(query_part, 'dp', scatter_dimension=0, tiled=True)  80 us
  transfers between devices with their start and end apart: 15, of which 14 were waited for; matrix products, arithmetic and copies ran while one was open for 6% of the time, Pallas kernels for 0%

commit v1 on v0

--- a/solution.py
+++ b/solution.py
@@ -163,7 +163,12 @@
     produced = jnp.einsum(
         "erh,ehd->erd", hidden, down_weight, preferred_element_type=jnp.float32
     ).astype(jnp.bfloat16)
-    returned = lax.all_to_all(produced, "expert", split_axis=1, concat_axis=0, tiled=True)
+    returned = jnp.concatenate(
+        lax.all_to_all(
+            jnp.stack(jnp.split(produced, lax.axis_size("expert"), axis=1)), "expert", 0, 0
+        ),
+        axis=0,
+    )
     picked = returned[flat, slots].reshape(token_rows, choices_per, width)
     combined = jnp.einsum("tk,tkd->td", gates, picked.astype(jnp.float32), precision=HIGHEST)
     layer_out = (resid + combined).astype(jnp.bfloat16)

time: 1810 us -> 1720 us (0.950)
  waiting for transfers between devices: 1130 us -> 1050 us
  local copies, waits for them, and re-layouts: 112 us -> 93.7 us
    all_to_all x1, waiting for transfers between devices: 194 us -> 118 us  [local(): lax.all_to_all(jnp.stack(jnp.split(produced, lax.axis_size('expert'), axi...]
where the time goes in v1:
time: 1720 us; the launch traced here: 1710 us
  waiting for transfers between devices  1050 us (61%)
  blocking collectives  335 us (19%)
  matrix products  163 us (9%)
  local copies, waits for them, and re-layouts  93.7 us (5%)
  other arithmetic  31.1 us (2%)
    all_to_all x1, waiting for transfers between devices, local(): lax.all_to_all(rows_back, 'expert', split_axis=1, concat_axis=0, tiled=True)  199 us
    all_to_all x1, blocking collectives, local(): lax.all_to_all(outgoing, 'expert', split_axis=0, concat_axis=1, tiled=True)  135 us
    all_to_all x1, blocking collectives, local(): lax.all_to_all(leaving, 'expert', split_axis=0, concat_axis=1, tiled=True)  133 us
    psum x1, waiting for transfers between devices, local(): lax.psum((partial_sums[0], partial_sums[1], partial_sums[2], partial_sums...  125 us
    all_to_all x1, waiting for transfers between devices, local(): lax.all_to_all(jnp.stack(jnp.split(produced, lax.axis_size('expert'), axi...  118 us
    reduce_scatter x1, waiting for transfers between devices, local(): lax.psum_scatter(up_part, 'dp', scatter_dimension=1, tiled=True)  113 us
    reduce_scatter x1, waiting for transfers between devices, local(): lax.psum_scatter(gate_part, 'dp', scatter_dimension=1, tiled=True)  113 us
    reduce_scatter x1, waiting for transfers between devices, local(): lax.psum_scatter(out_part, 'dp', scatter_dimension=0, tiled=True)  80 us
  transfers between devices with their start and end apart: 15, of which 14 were waited for; matrix products, arithmetic and copies ran while one was open for 6% of the time, Pallas kernels for 0%

profile of v1, /device:TPU:0, one launch (start us, length us, event | category | flops | bytes accessed | tf_op | source)
XLA Modules:
  0.0 1706.6 jit_solution(9802376331697893075)
XLA Ops:
  14.8 15.5 all-reduce.7
  40.5 25.7 %all-gather.8.cloned.1.call-done = bf16[1536,512]{1,0:T(8,128)(2,1)} async-done(((bf16[192,512]{1,0:T(8,128)(2,1)}), bf16[1536,512]{1,0:T(8,128)(2,1)}) %all-gather.8.cloned.1.call-update) | async-done | bytes 1572880 | tf_op jit(solution)/shard_map/all_gather | solution.py:93
  68.4 38.6 %all-gather.10.cloned.1.call-done = bf16[1536,1536]{1,0:T(8,128)(2,1)} async-done(((bf16[192,1536]{1,0:T(8,128)(2,1)}), bf16[1536,1536]{1,0:T(8,128)(2,1)}) %all-gather.10.cloned.1.call-update) | async-done | bytes 4718608 | tf_op jit(solution)/shard_map/all_gather | solution.py:92
  114.2 33.5 %all-gather.12.cloned.1.call-done = bf16[1536,1536]{1,0:T(8,128)(2,1)} async-done(((bf16[192,1536]{1,0:T(8,128)(2,1)}), bf16[1536,1536]{1,0:T(8,128)(2,1)}) %all-gather.12.cloned.1.call-update) | async-done | bytes 4718608 | tf_op jit(solution)/shard_map/all_gather | solution.py:95
  152.0 9.5 scatter_custom_fusion
  161.5 134.7 %all_to_all.59 = bf16[20,96,1536]{2,1,0:T(8,128)(2,1)S(1)} all-to-all(bf16[20,96,1536]{2,1,0:T(8,128)(2,1)} %bitcast.195), channel_id=1, replica_groups=mesh['dp'=8,'expert'=4] {'expert'}, dimensions={0} | all-to-all | bytes 11796480 | tf_op jit(solution)/shard_map/all_to_all | solution.py:161
  296.7 10.8 fusion.76
  330.6 9.3 all-gather
  341.9 117.9 %all-to-all-done.1 = bf16[4,5,96,1536]{3,2,1,0:T(8,128)(2,1)} async-done(((bf16[4,5,96,1536]{3,2,1,0:T(8,128)(2,1)}), bf16[4,5,96,1536]{3,2,1,0:T(8,128)(2,1)}, u32[]{:S(2)}, u32[]{:S(2)}) %all-to-all-start.1) | async-done | bytes 5898272 | tf_op jit(solution)/shard_map/all_to_all | solution.py:167
  459.9 17.8 %gather_fusion = bf16[1024,1536]{1,0:T(8,128)(2,1)S(1)} fusion(bf16[20,96,1536]{2,1,0:T(8,128)(2,1)} %bitcast.28, s32[1024]{0:T(1024)S(1)} %bitcast.183), kind=kCustom, calls=%fused_computation | custom fusion | bytes 6299648 | tf_op jit(solution)/shard_map/gather | solution.py:172
  483.8 9.6 scatter_custom_fusion.1
  493.4 133.4 %all_to_all.60 = bf16[20,96,1536]{2,1,0:T(8,128)(2,1)S(1)} all-to-all(bf16[20,96,1536]{2,1,0:T(8,128)(2,1)} %bitcast.192), channel_id=1, replica_groups=mesh['dp'=8,'expert'=4] {'expert'}, dimensions={0} | all-to-all | bytes 11796480 | tf_op jit(solution)/shard_map/all_to_all | solution.py:187
  629.9 12.5 multiply_convert_fusion
  642.4 11.2 fusion.77
  653.6 13.0 add_convert_fusion
  666.5 10.0 copy.106
  688.5 198.6 %all-to-all-done.3 = bf16[5,384,1536]{2,0,1:T(8,128)(2,1)} async-done(((bf16[5,384,1536]{2,0,1:T(8,128)(2,1)}), bf16[5,384,1536]{2,0,1:T(8,128)(2,1)}, u32[]{:S(2)}, u32[]{:S(2)}) %all-to-all-start.3) | async-done | bytes 5898272 | tf_op jit(solution)/shard_map/all_to_all | solution.py:210
  887.1 8.5 copy.107
  895.6 23.3 %gather_fusion.1 = bf16[1024,1536]{1,0:T(8,128)(2,1)} fusion(bf16[20,96,1536]{2,1,0:T(8,128)(2,1)} %bitcast.185, s32[1024]{0:T(1024)S(1)} %bitcast.184), kind=kCustom, calls=%fused_computation.1 | custom fusion | bytes 6299648 | tf_op jit(solution)/shard_map/gather | solution.py:212
  967.3 13.1 fusion.83
  980.6 13.8 fusion.82
  994.5 11.3 fusion.81
  1006.0 24.8 %reduce-scatter.13.cloned.1.call-done = f32[192,512]{1,0:T(8,128)} async-done(((f32[1536,512]{1,0:T(8,128)}), f32[192,512]{1,0:T(8,128)}) %reduce-scatter.13.cloned.1.call-update) | async-done | bytes 393232 | tf_op jit(solution)/shard_map/reduce_scatter | solution.py:271
  1030.7 80.0 %reduce-scatter.17.cloned.1.call-done = f32[192,1536]{1,0:T(8,128)} async-done(((f32[1536,1536]{1,0:T(8,128)}), f32[192,1536]{1,0:T(8,128)}) %reduce-scatter.17.cloned.1.call-update) | async-done | bytes 1179664 | tf_op jit(solution)/shard_map/reduce_scatter | solution.py:273
  1110.7 80.0 %reduce-scatter.11.cloned.1.call-done = f32[192,1536]{1,0:T(8,128)} async-done(((f32[1536,1536]{1,0:T(8,128)}), f32[192,1536]{1,0:T(8,128)}) %reduce-scatter.11.cloned.1.call-update) | async-done | bytes 1179664 | tf_op jit(solution)/shard_map/reduce_scatter | solution.py:270
  1191.6 37.9 %reduce-scatter.25.cloned.1.call-done = f32[192,20]{1,0:T(8,128)} async-done(((f32[1536,20]{1,0:T(8,128)}), f32[192,20]{1,0:T(8,128)}) %reduce-scatter.25.cloned.1.call-update) | async-done | bytes 15376
  1236.2 22.8 %all-reduce.4 = (f32[1536]{0:T(1024)S(1)}, f32[1536]{0:T(1024)S(1)}) all-reduce(f32[1536]{0:T(1024)S(1)} %get-tuple-element.14, f32[1536]{0:T(1024)S(1)} %copy-done.47), channel_id=6, replica_groups=mesh['dp'=8,'expert'=4] {'dp'}, use_global_device_ids=true, to_apply=%region_28.29.clone | all-reduce | flops 3072 | bytes 24576
  1259.1 19.6 %all-reduce.5 = (f32[192]{0:T(256)}, f32[192]{0:T(256)}, f32[192,20]{0,1:T(8,128)}) all-reduce(f32[192]{0:T(256)S(1)} %dynamic-slice.3, f32[192]{0:T(256)S(1)} %dynamic-slice.5, f32[192,20]{0,1:T(8,128)S(1)} %copy.133), channel_id=1, replica_groups=mesh['dp'=8,'expert'=4] {'expert'}, use_global_device_ids=true, to_apply=%region_29.30 | all-reduce | flops 4224 | bytes 33792 | tf_op jit(solution)/shard_map/psum | solution.py:278
  1279.9 62.7 %reduce-scatter.23.cloned.1.call-done = f32[5,64,1536]{2,1,0:T(8,128)} async-done(((f32[5,512,1536]{2,1,0:T(8,128)}), f32[5,64,1536]{2,1,0:T(8,128)}) %reduce-scatter.23.cloned.1.call-update) | async-done | bytes 1966096 | tf_op jit(solution)/shard_map/reduce_scatter | solution.py:293
  1342.6 113.3 %reduce-scatter.21.cloned.1.call-done = f32[5,192,512]{2,1,0:T(8,128)} async-done(((f32[5,1536,512]{2,1,0:T(8,128)}), f32[5,192,512]{2,1,0:T(8,128)}) %reduce-scatter.21.cloned.1.call-update) | async-done | bytes 1966096 | tf_op jit(solution)/shard_map/reduce_scatter | solution.py:292
  1455.9 113.1 %reduce-scatter.19.cloned.1.call-done = f32[5,192,512]{2,1,0:T(8,128)} async-done(((f32[5,1536,512]{2,1,0:T(8,128)}), f32[5,192,512]{2,1,0:T(8,128)}) %reduce-scatter.19.cloned.1.call-update) | async-done | bytes 1966096 | tf_op jit(solution)/shard_map/reduce_scatter | solution.py:291
  1569.1 124.8 %all-reduce.10.cloned.1.call-done = (f32[192,1536]{1,0:T(8,128)}, f32[192,512]{1,0:T(8,128)}, f32[192,512]{1,0:T(8,128)}, f32[192,1536]{1,0:T(8,128)}) async-done(((f32[192,1536]{1,0:T(8,128)}, f32[192,512]{1,0:T(8,128)}, f32[192,512]{1,0:T(8,128)}, f32[192,1536]{1,0:T(8,128)}), (f32[192,1536]{1,0:T(8,128)}, f32[192,512]{1,0:T(8,128)}, f32[192,512]{1,0:T(8,128)}, ...) | async-done | bytes 3145744 | tf_op jit(solution)/shard_map/psum | solution.py:278
  (254 shorter events, 139.5 us)
Async XLA Ops:
  7.2 31.3 %all-gather.6.cloned.1.call-start = ((), (), s32[]{:S(2)}) async-start(), calls=%async_computation.12 | async-start | bytes 1769472 | tf_op jit(solution)/shard_map/all_gather | solution.py:94
  8.0 58.2 %all-gather.8.cloned.1.call-start = ((), (), s32[]{:S(2)}) async-start(), calls=%async_computation.13 | async-start | bytes 1769472 | tf_op jit(solution)/shard_map/all_gather | solution.py:93
  8.7 98.3 %all-gather.10.cloned.1.call-start = ((), (), s32[]{:S(2)}) async-start(), calls=%async_computation.14 | async-start | bytes 5308416 | tf_op jit(solution)/shard_map/all_gather | solution.py:92
  9.4 138.2 %all-gather.12.cloned.1.call-start = ((), (), s32[]{:S(2)}) async-start(), calls=%async_computation.15 | async-start | bytes 5308416 | tf_op jit(solution)/shard_map/all_gather | solution.py:95
  30.4 121.2 %copy-start.37 = (f32[1536]{0:T(1024)}, f32[1536]{0:T(1024)S(1)}, u32[]{:S(2)}) copy-start(f32[1536]{0:T(1024)S(1)} %convert_element_type.119) | copy-start | bytes 18436
  37.6 73.7 %copy-start.48 = (f32[128]{0:T(128)}, f32[128]{0:T(128)S(1)}, u32[]{:S(2)}) copy-start(f32[128]{0:T(128)S(1)} %get-tuple-element.53) | copy-start | bytes 1540
  37.6 114.3 %copy-start.54 = (s32[1024]{0:T(1024)}, s32[1024]{0:T(1024)S(1)}, u32[]{:S(2)}) copy-start(s32[1024]{0:T(1024)S(1)} %broadcast_select_fusion) | copy-start | bytes 12292
  37.9 73.5 %copy-start.26 = (f32[128,32]{0,1:T(8,128)}, f32[128,32]{0,1:T(8,128)S(1)}, u32[]{:S(2)}) copy-start(f32[128,32]{0,1:T(8,128)S(1)} %get-tuple-element.48) | copy-start | bytes 49156
  37.9 73.5 %copy-start.29 = (f32[128,32]{0,1:T(8,128)}, f32[128,32]{0,1:T(8,128)S(1)}, u32[]{:S(2)}) copy-start(f32[128,32]{0,1:T(8,128)S(1)} %get-tuple-element.49) | copy-start | bytes 49156
  40.5 72.5 %copy-start.20 = (bf16[128,512]{0,1:T(8,128)(2,1)}, bf16[128,512]{0,1:T(8,128)(2,1)S(1)}, u32[]{:S(2)}) copy-start(bf16[128,512]{0,1:T(8,128)(2,1)S(1)} %copy.93) | copy-start | bytes 393220
  68.4 43.1 %copy-start.40 = (bf16[128,8,32]{0,2,1:T(8,128)(2,1)}, bf16[128,8,32]{0,2,1:T(8,128)(2,1)S(1)}, u32[]{:S(2)}) copy-start(bf16[128,8,32]{0,2,1:T(8,128)(2,1)S(1)} %get-tuple-element.43) | copy-start | bytes 196612
  68.4 43.1 %copy-start.42 = (bf16[128,8,32]{0,2,1:T(8,128)(2,1)}, bf16[128,8,32]{0,2,1:T(8,128)(2,1)S(1)}, u32[]{:S(2)}) copy-start(bf16[128,8,32]{0,2,1:T(8,128)(2,1)S(1)} %get-tuple-element.44) | copy-start | bytes 196612
  114.2 36.8 %copy-start.9 = (bf16[8,64,3,128]{3,1,2,0:T(8,128)(2,1)}, bf16[8,64,3,128]{3,1,2,0:T(8,128)(2,1)S(1)}, u32[]{:S(2)}) copy-start(bf16[8,64,3,128]{3,1,2,0:T(8,128)(2,1)S(1)} %convolution_convert_fusion.2) | copy-start | bytes 1179652
  152.0 189.1 %copy-start.7 = (bf16[128,1536]{1,0:T(8,128)(2,1)}, bf16[128,1536]{1,0:T(8,128)(2,1)S(1)}, u32[]{:S(2)}) copy-start(bf16[128,1536]{1,0:T(8,128)(2,1)S(1)} %multiply_convert_fusion.3) | copy-start | bytes 1179652
  325.3 134.6 %all-to-all-start.1 = ((bf16[4,5,96,1536]{3,2,1,0:T(8,128)(2,1)}), bf16[4,5,96,1536]{3,2,1,0:T(8,128)(2,1)}, u32[]{:S(2)}, u32[]{:S(2)}) async-start(bf16[4,5,96,1536]{3,2,1,0:T(8,128)(2,1)} %pad_maximum_fusion), calls=%async_computation.1 | async-start | bytes 11796480 | tf_op jit(solution)/shard_map/all_to_all | solution.py:167
  340.1 119.8 %copy-start.24 = (bf16[1536,20]{0,1:T(8,128)(2,1)}, bf16[1536,20]{0,1:T(8,128)(2,1)S(1)}, u32[]{:S(2)}) copy-start(bf16[1536,20]{0,1:T(8,128)(2,1)S(1)} %reshape.372) | copy-start | bytes 184324
  341.3 118.6 %copy-start.53 = (f32[128]{0:T(128)}, f32[128]{0:T(128)S(1)}, u32[]{:S(2)}) copy-start(f32[128]{0:T(128)S(1)} %reduce_max.19) | copy-start | bytes 1540
  676.5 210.6 %all-to-all-start.3 = ((bf16[5,384,1536]{2,0,1:T(8,128)(2,1)}), bf16[5,384,1536]{2,0,1:T(8,128)(2,1)}, u32[]{:S(2)}, u32[]{:S(2)}) async-start(bf16[5,384,1536]{2,0,1:T(8,128)(2,1)} %copy.106), calls=%async_computation.3 | async-start | bytes 18874368 | tf_op jit(solution)/shard_map/all_to_all | solution.py:210
  682.5 323.5 %reduce-scatter.15.cloned.1.call-start = ((), (), s32[]{:S(2)}) async-start(), calls=%async_computation.18 | async-start | bytes 3538944 | tf_op jit(solution)/shard_map/reduce_scatter | solution.py:272
  683.1 239.9 %copy-start.39 = (f32[128,20]{0,1:T(8,128)}, f32[128,20]{0,1:T(8,128)S(1)}, u32[]{:S(2)}) copy-start(f32[128,20]{0,1:T(8,128)S(1)} %select_reduce_fusion) | copy-start | bytes 30724
  936.3 94.4 %reduce-scatter.13.cloned.1.call-start = ((), (), s32[]{:S(2)}) async-start(), calls=%async_computation.17 | async-start | bytes 3538944 | tf_op jit(solution)/shard_map/reduce_scatter | solution.py:271
  946.5 164.2 %reduce-scatter.17.cloned.1.call-start = ((), (), s32[]{:S(2)}) async-start(), calls=%async_computation.19 | async-start | bytes 10616832 | tf_op jit(solution)/shard_map/reduce_scatter | solution.py:273
  951.5 239.2 %reduce-scatter.11.cloned.1.call-start = ((), (), s32[]{:S(2)}) async-start(), calls=%async_computation.16 | async-start | bytes 10616832 | tf_op jit(solution)/shard_map/reduce_scatter | solution.py:270
  964.1 265.4 %reduce-scatter.25.cloned.1.call-start = ((), (), s32[]{:S(2)}) async-start(), calls=%async_computation.23 | async-start | bytes 884736
  967.2 375.4 %reduce-scatter.23.cloned.1.call-start = ((), (), s32[]{:S(2)}) async-start(), calls=%async_computation.22 | async-start | bytes 17694720 | tf_op jit(solution)/shard_map/reduce_scatter | solution.py:293
  980.4 475.6 %reduce-scatter.21.cloned.1.call-start = ((), (), s32[]{:S(2)}) async-start(), calls=%async_computation.21 | async-start | bytes 17694720 | tf_op jit(solution)/shard_map/reduce_scatter | solution.py:292
  994.5 574.6 %reduce-scatter.19.cloned.1.call-start = ((), (), s32[]{:S(2)}) async-start(), calls=%async_computation.20 | async-start | bytes 17694720 | tf_op jit(solution)/shard_map/reduce_scatter | solution.py:291
  1005.9 224.6 %copy-start.12 = (bf16[128,24,64]{0,2,1:T(8,128)(2,1)S(1)}, bf16[128,24,64]{0,2,1:T(8,128)(2,1)}, u32[]{:S(2)}) copy-start(bf16[128,24,64]{0,2,1:T(8,128)(2,1)} %copy-done.11) | copy-start | bytes 1179652
  1005.9 687.9 %all-reduce.10.cloned.1.call-start = ((), (), s32[]{:S(2)}) async-start(), calls=%async_computation.24 | async-start | bytes 6291456 | tf_op jit(solution)/shard_map/psum | solution.py:278
  1190.8 43.9 %copy-start.6 = (bf16[1536,512]{1,0:T(8,128)(2,1)S(1)}, bf16[1536,512]{1,0:T(8,128)(2,1)}, u32[]{:S(2)}) copy-start(bf16[1536,512]{1,0:T(8,128)(2,1)} %all-gather.8.cloned.1.call-done) | copy-start | bytes 4718596
  1190.8 43.9 %copy-start.22 = (bf16[128,8,64]{0,2,1:T(8,128)(2,1)S(1)}, bf16[128,8,64]{0,2,1:T(8,128)(2,1)}, u32[]{:S(2)}) copy-start(bf16[128,8,64]{0,2,1:T(8,128)(2,1)} %copy-done.21) | copy-start | bytes 393220
  1234.7 44.0 %copy-start.59 = (f32[128]{0:T(128)S(1)}, f32[128]{0:T(128)}, u32[]{:S(2)}) copy-start(f32[128]{0:T(128)} %get-tuple-element.52) | copy-start | bytes 1540
  (45 other events, 316.0 us)
Sparse Core Ops, SparseCore 0:
  9.9 28.5 all-gather.5
  40.4 25.7 all-gather.7
  68.0 38.9 all-gather.9
  108.7 38.9 all-gather.11
  936.5 44.3 reduce-scatter.14
  984.5 46.1 reduce-scatter.12
  1034.2 76.4 reduce-scatter.16
  1114.2 76.4 reduce-scatter.10
  1194.5 34.9 reduce-scatter.24
  1233.4 109.1 reduce-scatter.22
  1346.7 109.1 reduce-scatter.20
  1459.8 109.1 reduce-scatter.18
  1571.7 122.1 all-reduce.9
